TPU v7x, 32 devices: a whole 2x2x4 slice. The times are simulated.
32 devices in a mesh: replica: 8 (over z, core), shard: 4 (over y, x).
Axes of the slice: x: 2, y: 2, z: 4, core: 2. Of those that a mesh axis runs over, the one named last changes fastest.
Arguments:
- local_weights: bfloat16 [8, 8192, 512], P('replica', 'shard'), may hold values from -1.3258252 to 1.3258252
- outer_base: bfloat16 [8192, 512], P('shard'), may hold values from -0.0625 to 0.0625
- momentum: bfloat16 [8192, 512], P('shard', 'replica'), may hold values from -0.06591797 to 0.06591797
- error_feedback: bfloat16 [8, 8192, 512], P('replica', 'shard'), may hold values from -0.032958984 to 0.032958984
- q_start: float32 [512, 32], replicated, may hold values from -6 to 6
- tokens: bfloat16 [8, 512, 8192], P('replica', None, 'shard'), may hold values from -6 to 6
Outputs:
- new_base: bfloat16 [8192, 512], P('shard')
- new_momentum: bfloat16 [8192, 512], P('shard', 'replica')
- new_error: bfloat16 [8, 8192, 512], P('replica', 'shard')
- key_rows: bfloat16 [8, 512, 512], P('replica', 'shard')
All inputs are finite; a program needn't handle non-finite values.
Results may differ from a plain program's by a relative error of at most 0.0065.
Values may be sent and summed in bfloat16 or wider, within the bound.
A program may use at most 64 MiB of HBM per device.

v0:
```python
import jax
import jax.numpy as jnp
from jax import lax
from jax.sharding import PartitionSpec as P

outer_mu = 0.9
outer_rate = 0.7


def on_device(local_weights, outer_base, momentum, error_feedback, q_start, tokens):
    highest = lax.Precision.HIGHEST
    replicas = lax.axis_size("replica")
    own_columns = momentum.shape[1]
    full_momentum = lax.all_gather(momentum, "replica", axis=1, tiled=True)
    pseudo = (
        outer_base.astype(jnp.float32)
        - local_weights[0].astype(jnp.float32)
        + error_feedback[0].astype(jnp.float32)
    )
    p_local = jnp.dot(pseudo, q_start, precision=highest)
    p_mean = lax.psum(p_local, "replica") / replicas
    own_gram = jnp.dot(p_mean.T, p_mean, precision=highest)
    gram_sum = lax.psum(own_gram, "shard")
    factor_low = jnp.linalg.cholesky(gram_sum)
    basis = jax.scipy.linalg.solve_triangular(factor_low, p_mean.T, lower=True).T
    q_raw = jnp.dot(pseudo.T, basis, precision=highest)
    q_mean = lax.psum(q_raw, ("replica", "shard")) / replicas
    update = jnp.dot(basis, q_mean.T, precision=highest)
    new_error = (pseudo - update).astype(jnp.bfloat16)[None]
    moment = outer_mu * full_momentum.astype(jnp.float32) + update
    new_base = (outer_base.astype(jnp.float32) - outer_rate * (outer_mu * moment + update)).astype(
        jnp.bfloat16
    )
    first_column = lax.axis_index("replica") * own_columns
    new_momentum = lax.dynamic_slice_in_dim(moment, first_column, own_columns, 1).astype(
        jnp.bfloat16
    )
    own_tokens = tokens[0]
    key_sum = lax.psum_scatter(
        jnp.dot(own_tokens, new_base, preferred_element_type=jnp.float32),
        "shard",
        scatter_dimension=0,
        tiled=True,
    )
    key_rows = key_sum.astype(jnp.bfloat16)[None]
    return (new_base, new_momentum, new_error, key_rows)


def solution(mesh):
    in_specs = (
        P("replica", "shard", None),
        P("shard", None),
        P("shard", "replica"),
        P("replica", "shard", None),
        P(),
        P("replica", None, "shard"),
    )
    out_specs = (
        P("shard", None),
        P("shard", "replica"),
        P("replica", "shard", None),
        P("replica", "shard", None),
    )
    return jax.shard_map(
        on_device, mesh=mesh, in_specs=in_specs, out_specs=out_specs, check_vma=False
    )
```

profile of v0, /device:TPU:0, one launch (start us, length us, event | category | flops | bytes accessed | tf_op | source)
XLA Modules:
  0.0 319.2 jit_solution(3947755793024692435)
XLA Ops:
  7.2 0.0 copy-start
  7.2 0.0 all-reduce.3.cloned.1.call-start
  7.2 4.1 %copy.10 = bf16[2048,512]{0,1:T(8,128)(2,1)} copy(bf16[2048,512]{1,0:T(8,128)(2,1)} %param.7) | data formatting | bytes 4194304 | tf_op args[1]
  11.3 4.0 %copy.11 = bf16[1,2048,512]{1,2,0:T(8,128)(2,1)} copy(bf16[1,2048,512]{2,1,0:T(8,128)(2,1)} %param.6) | data formatting | bytes 4194304 | tf_op args[0]
  15.3 0.0 copy-start.6
  15.3 3.9 %copy.12 = bf16[1,2048,512]{1,2,0:T(8,128)(2,1)} copy(bf16[1,2048,512]{2,1,0:T(8,128)(2,1)} %param.9) | data formatting | bytes 4194304 | tf_op args[3]
  19.2 0.0 copy-done.6
  19.2 6.8 %fusion.10 = f32[2048,32]{0,1:T(8,128)} fusion(f32[512,32]{0,1:T(8,128)S(1)} %copy-done.6, bf16[2048,512]{0,1:T(8,128)(2,1)} %copy.10, bf16[1,2048,512]{1,2,0:T(8,128)(2,1)} %copy.12, bf16[1,2048,512]{1,2,0:T(8,128)(2,1)} %copy.11), kind=kOutput, calls=%fused_computation.11 | convolution fusion | flops 407896064 | bytes 6619136 | tf_op jit(solution)/shard_map/dot_general | solution.py:20
  26.0 0.0 all-reduce.3.cloned.1.call-update
  26.0 0.0 all-reduce.5.cloned.1.call-start
  26.1 58.3 %all-reduce.3.cloned.1.call-done = f32[2048,32]{0,1:T(8,128)} async-done(((f32[2048,32]{0,1:T(8,128)}), f32[2048,32]{0,1:T(8,128)}) %all-reduce.3.cloned.1.call-update) | async-done | bytes 262160 | tf_op jit(solution)/shard_map/psum | solution.py:21
  84.3 1.4 fusion.16
  85.7 16.0 %psum.22 = f32[32,32]{0,1:T(8,128)S(1)} all-reduce(f32[32,32]{0,1:T(8,128)S(1)} %fusion.16), channel_id=1, replica_groups=mesh['replica'=8,'shard'=4] {'shard'}, use_global_device_ids=true, to_apply=%region_1.0 | all-reduce | flops 1024 | bytes 8192 | tf_op jit(solution)/shard_map/psum | solution.py:23
  101.7 0.1 copy.14
  101.8 2.9 cholesky.16
  104.7 0.6 compare_reduce_fusion
  105.4 0.7 fusion.21
  106.0 2.4 custom-call.7
  108.4 1.4 fusion.14
  109.8 6.4 %fusion.8 = f32[512,32]{1,0:T(8,128)} fusion(f32[32,2048]{1,0:T(8,128)S(1)} %fusion.14, bf16[2048,512]{0,1:T(8,128)(2,1)} %copy.10, bf16[1,2048,512]{1,2,0:T(8,128)(2,1)} %copy.12, bf16[1,2048,512]{1,2,0:T(8,128)(2,1)} %copy.11), kind=kOutput, calls=%fused_computation.10 | convolution fusion | flops 407896064 | bytes 6619136 | tf_op jit(solution)/shard_map/dot_general | solution.py:26
  116.2 0.0 all-reduce.5.cloned.1.call-update
  116.3 0.0 all-gather.2.cloned.1.call-start
  116.3 0.7 all-gather.2.cloned.1.call-update
  117.0 0.2 reduce-scatter.2.cloned.1.call-start
  117.2 123.0 %all-reduce.5.cloned.1.call-done = f32[512,32]{1,0:T(8,128)} async-done(((f32[512,32]{1,0:T(8,128)}), f32[512,32]{1,0:T(8,128)}) %all-reduce.5.cloned.1.call-update) | async-done | bytes 65552 | tf_op jit(solution)/shard_map/psum | solution.py:27
  240.2 29.8 %all-gather.2.cloned.1.call-done = bf16[2048,512]{0,1:T(8,128)(2,1)} async-done(((bf16[2048,64]{0,1:T(8,128)(2,1)}), bf16[2048,512]{0,1:T(8,128)(2,1)}) %all-gather.2.cloned.1.call-update) | async-done | bytes 2097168 | tf_op jit(solution)/shard_map/all_gather | solution.py:14
  270.1 0.0 copy-start.1
  270.1 0.0 copy-start.2
  270.1 0.0 copy-start.3
  270.1 0.0 copy-start.4
  270.1 6.3 %multiply_add_fusion = (bf16[2048,512]{0,1:T(8,128)(2,1)}, f32[2048,512]{0,1:T(8,128)S(1)}) fusion(bf16[2048,512]{0,1:T(8,128)(2,1)} %all-gather.2.cloned.1.call-done, f32[32,2048]{1,0:T(8,128)S(1)} %fusion.14, f32[512,32]{1,0:T(8,128)} %all-reduce.5.cloned.1.call-done), kind=kOutput, calls=%fused_computation.5 | convolution fusion | flops 406863872 | bytes 8716288 | tf_op jit(solution)/shard_map/dot_general | solution.py:28
  276.4 0.0 copy-done.1
  276.4 0.0 copy-done.2
  276.4 0.0 copy-done.3
  276.4 0.0 copy-done.4
  276.4 3.5 %fusion.2 = (bf16[1,2048,512]{1,2,0:T(8,128)(2,1)}, bf16[2048,512]{0,1:T(8,128)(2,1)S(1)}) fusion(f32[2048,512]{0,1:T(8,128)S(1)} %get-tuple-element.11, bf16[1,2048,512]{1,2,0:T(8,128)(2,1)S(1)} %copy-done.3, bf16[1,2048,512]{1,2,0:T(8,128)(2,1)S(1)} %copy-done.2, bf16[2048,512]{0,1:T(8,128)(2,1)S(1)} %copy-done.1, bf16[2048,512]{0,1:T(8,128)(2,1)S(1)} %copy-done.4), kind=kLoop, calls=%fused_computation.6 | loop fusion | flops 15728640 | bytes 16777216 | tf_op jit(solution)/shard_map/broadcast_in_dim | solution.py:29
  279.8 0.0 copy-start.5
  279.9 1.3 copy-done.5
  281.2 0.0 copy-done
  281.2 2.3 fusion.5
  283.4 0.0 reduce-scatter.2.cloned.1.call-update
  283.5 3.9 %copy.15 = bf16[2048,512]{1,0:T(8,128)(2,1)} copy(bf16[2048,512]{0,1:T(8,128)(2,1)} %copy-done.5) | data formatting | bytes 4194304
  287.4 4.0 %copy.16 = bf16[1,2048,512]{2,1,0:T(8,128)(2,1)} copy(bf16[1,2048,512]{1,2,0:T(8,128)(2,1)} %get-tuple-element.8) | data formatting | bytes 4194304
  291.3 1.7 dynamic-slice_convert_fusion
  293.0 17.9 %reduce-scatter.2.cloned.1.call-done = f32[128,512]{0,1:T(8,128)} async-done(((f32[512,512]{0,1:T(8,128)}), f32[128,512]{0,1:T(8,128)}) %reduce-scatter.2.cloned.1.call-update) | async-done | bytes 262160 | tf_op jit(solution)/shard_map/reduce_scatter | solution.py:39
  310.9 1.0 convert_bitcast_fusion
  311.9 0.8 copy.17
  (2 shorter events, 0.0 us)
Async XLA Ops:
  7.2 274.0 %copy-start = (bf16[1,512,2048]{2,1,0:T(8,128)(2,1)S(1)}, bf16[1,512,2048]{2,1,0:T(8,128)(2,1)}, u32[]{:S(2)}) copy-start(bf16[1,512,2048]{2,1,0:T(8,128)(2,1)} %param.11) | copy-start | bytes 6291460
  7.2 77.1 %all-reduce.3.cloned.1.call-start = ((), (), s32[]{:S(2)}) async-start(), calls=%async_computation.2 | async-start | bytes 524288 | tf_op jit(solution)/shard_map/psum | solution.py:21
  15.3 3.9 %copy-start.6 = (f32[512,32]{0,1:T(8,128)S(1)}, f32[512,32]{0,1:T(8,128)}, u32[]{:S(2)}) copy-start(f32[512,32]{0,1:T(8,128)} %param.10) | copy-start | bytes 196612
  26.0 214.2 %all-reduce.5.cloned.1.call-start = ((), (), s32[]{:S(2)}) async-start(), calls=%async_computation.3 | async-start | bytes 524288 | tf_op jit(solution)/shard_map/psum | solution.py:27
  116.3 153.8 %all-gather.2.cloned.1.call-start = ((), (), s32[]{:S(2)}) async-start(), calls=%async_computation.1 | async-start | bytes 2359296 | tf_op jit(solution)/shard_map/all_gather | solution.py:14
  117.0 193.9 %reduce-scatter.2.cloned.1.call-start = ((), (), s32[]{:S(2)}) async-start(), calls=%async_computation.4 | async-start | bytes 1310720 | tf_op jit(solution)/shard_map/reduce_scatter | solution.py:39
  270.1 6.3 %copy-start.1 = (bf16[2048,512]{0,1:T(8,128)(2,1)S(1)}, bf16[2048,512]{0,1:T(8,128)(2,1)}, u32[]{:S(2)}) copy-start(bf16[2048,512]{0,1:T(8,128)(2,1)} %copy.10) | copy-start | bytes 6291460
  270.1 6.3 %copy-start.2 = (bf16[1,2048,512]{1,2,0:T(8,128)(2,1)S(1)}, bf16[1,2048,512]{1,2,0:T(8,128)(2,1)}, u32[]{:S(2)}) copy-start(bf16[1,2048,512]{1,2,0:T(8,128)(2,1)} %copy.11) | copy-start | bytes 6291460
  270.1 6.3 %copy-start.3 = (bf16[1,2048,512]{1,2,0:T(8,128)(2,1)S(1)}, bf16[1,2048,512]{1,2,0:T(8,128)(2,1)}, u32[]{:S(2)}) copy-start(bf16[1,2048,512]{1,2,0:T(8,128)(2,1)} %copy.12) | copy-start | bytes 6291460
  270.1 6.3 %copy-start.4 = (bf16[2048,512]{0,1:T(8,128)(2,1)S(1)}, bf16[2048,512]{0,1:T(8,128)(2,1)}, u32[]{:S(2)}) copy-start(bf16[2048,512]{0,1:T(8,128)(2,1)} %all-gather.2.cloned.1.call-done) | copy-start | bytes 6291460
  279.8 1.3 copy-start.5
Sparse Core Ops, SparseCore 0:
  26.1 58.1 all-reduce.2
  116.4 123.7 all-reduce.4
  241.8 28.1 all-gather.1
  283.6 27.3 reduce-scatter.1
where the time goes:
time: 320 us; the launch traced here: 319 us
  waiting for transfers between devices  230 us (72%)
  matrix products  24.5 us (8%)
  local copies, waits for them, and re-layouts  23.7 us (7%)
  blocking collectives  16 us (5%)
  between operations  13.8 us (4%)
  other arithmetic  11.1 us (3%)
    psum x1, waiting for transfers between devices, on_device(): q_mean = lax.psum(q_raw, ('replica', 'shard')) / replicas  123 us
    psum x1, waiting for transfers between devices, on_device(): p_mean = lax.psum(p_local, 'replica') / replicas  58.3 us
    all_gather x1, waiting for transfers between devices, on_device(): full_momentum = lax.all_gather(momentum, 'replica', axis=1, tiled=True)  29.8 us
    unnamed x20, local copies, waits for them, and re-layouts  22 us
    reduce_scatter x1, waiting for transfers between devices, on_device(): lax.psum_scatter(jnp.dot(own_tokens, new_base, preferred_element_type=jnp...  17.9 us
    psum x1, blocking collectives, on_device(): gram_sum = lax.psum(own_gram, 'shard')  16 us
    dot_general x1, matrix products, on_device(): p_local = jnp.dot(pseudo, q_start, precision=highest)  6.77 us
  transfers between devices with their start and end apart: 4, of which 4 were waited for; matrix products, arithmetic and copies ran while one was open for 3% of the time, Pallas kernels for 0%

commit v1 on v0

--- a/solution.py
+++ b/solution.py
@@ -11,7 +11,13 @@
     highest = lax.Precision.HIGHEST
     replicas = lax.axis_size("replica")
     own_columns = momentum.shape[1]
-    full_momentum = lax.all_gather(momentum, "replica", axis=1, tiled=True)
+    size = lax.axis_size("replica")
+    held, blocks = (momentum, [momentum])
+    for _ in range(size - 1):
+        held = lax.ppermute(held, "replica", [(i, (i + 1) % size) for i in range(size)])
+        blocks.insert(0, held)
+    line = jnp.concatenate(blocks, axis=1)
+    full_momentum = jnp.roll(line, (lax.axis_index("replica") + 1) * momentum.shape[1], axis=1)
     pseudo = (
         outer_base.astype(jnp.float32)
         - local_weights[0].astype(jnp.float32)

time: 320 us -> 309 us (0.966)
  waiting for transfers between devices: 230 us -> 198 us
  local copies, waits for them, and re-layouts: 23.7 us -> 41.6 us
    all_gather x1 -> x0, waiting for transfers between devices: 29.8 us -> none  [on_device(): full_momentum = lax.all_gather(momentum, 'replica', axis=1, tiled=True)]
    ppermute x0 -> x7, waiting for transfers between devices: none -> 17.4 us  [on_device(): lax.ppermute(held, 'replica', [(i, (i + 1) % size) for i in range(size)])]
    unnamed x20 -> x39, local copies, waits for them, and re-layouts: 22 us -> 39.2 us
    psum x1, waiting for transfers between devices: 123 us -> 106 us  [on_device(): q_mean = lax.psum(q_raw, ('replica', 'shard')) / replicas]
  transfers between devices with their start and end apart: 4 -> 10, of which waited for: 4 -> 8; matrix products, arithmetic and copies ran while one was open for 3% -> 20% of each run, Pallas kernels for 0% -> 0%
where the time goes in v1:
time: 309 us; the launch traced here: 308 us
  waiting for transfers between devices  198 us (64%)
  local copies, waits for them, and re-layouts  41.6 us (13%)
  matrix products  24.5 us (8%)
  blocking collectives  16 us (5%)
  between operations  13.9 us (4%)
  other arithmetic  12.3 us (4%)
    psum x1, waiting for transfers between devices, on_device(): q_mean = lax.psum(q_raw, ('replica', 'shard')) / replicas  106 us
    psum x1, waiting for transfers between devices, on_device(): p_mean = lax.psum(p_local, 'replica') / replicas  56.9 us
    unnamed x39, local copies, waits for them, and re-layouts  39.2 us
    reduce_scatter x1, waiting for transfers between devices, on_device(): lax.psum_scatter(jnp.dot(own_tokens, new_base, preferred_element_type=jnp...  17.6 us
    ppermute x7, waiting for transfers between devices, on_device(): lax.ppermute(held, 'replica', [(i, (i + 1) % size) for i in range(size)])  17.4 us
    psum x1, blocking collectives, on_device(): gram_sum = lax.psum(own_gram, 'shard')  16 us
    dot_general x1, matrix products, on_device(): p_local = jnp.dot(pseudo, q_start, precision=highest)  6.77 us
    dot_general x1, matrix products, on_device(): q_raw = jnp.dot(pseudo.T, basis, precision=highest)  6.39 us
  transfers between devices with their start and end apart: 10, of which 8 were waited for; matrix products, arithmetic and copies ran while one was open for 20% of the time, Pallas kernels for 0%

profile of v1, /device:TPU:0, one launch (start us, length us, event | category | flops | bytes accessed | tf_op | source)
XLA Modules:
  0.0 307.9 jit_solution(5158362055439508418)
XLA Ops:
  7.2 0.5 collective-permute-start
  7.8 8.3 %collective-permute-done = bf16[2048,64]{0,1:T(8,128)(2,1)S(1)} collective-permute-done((bf16[2048,64]{0,1:T(8,128)(2,1)}, bf16[2048,64]{0,1:T(8,128)(2,1)S(1)}, u32[]{:S(2)}, u32[]{:S(2)}) %collective-permute-start) | collective-permute-done | bytes 262176 | tf_op jit(solution)/shard_map/ppermute | solution.py:17
  16.1 4.0 %copy.11 = bf16[1,2048,512]{1,2,0:T(8,128)(2,1)} copy(bf16[1,2048,512]{2,1,0:T(8,128)(2,1)} %param.6) | data formatting | bytes 4194304 | tf_op args[0]
  20.0 3.9 %copy.10 = bf16[2048,512]{0,1:T(8,128)(2,1)} copy(bf16[2048,512]{1,0:T(8,128)(2,1)} %param.7) | data formatting | bytes 4194304 | tf_op args[1]
  24.0 3.9 %copy.12 = bf16[1,2048,512]{1,2,0:T(8,128)(2,1)} copy(bf16[1,2048,512]{2,1,0:T(8,128)(2,1)} %param.9) | data formatting | bytes 4194304 | tf_op args[3]
  27.9 0.4 collective-permute-start.2
  28.3 6.8 %fusion.10 = f32[2048,32]{0,1:T(8,128)} fusion(f32[512,32]{0,1:T(8,128)S(1)} %copy-done.8, bf16[2048,512]{0,1:T(8,128)(2,1)} %copy.10, bf16[1,2048,512]{1,2,0:T(8,128)(2,1)} %copy.12, bf16[1,2048,512]{1,2,0:T(8,128)(2,1)} %copy.11), kind=kOutput, calls=%fused_computation.11 | convolution fusion | flops 407896064 | bytes 6619136 | tf_op jit(solution)/shard_map/dot_general | solution.py:26
  35.1 0.4 collective-permute-done.2
  35.5 56.9 %all-reduce.3.cloned.1.call-done = f32[2048,32]{0,1:T(8,128)} async-done(((f32[2048,32]{0,1:T(8,128)}), f32[2048,32]{0,1:T(8,128)}) %all-reduce.3.cloned.1.call-update) | async-done | bytes 262160 | tf_op jit(solution)/shard_map/psum | solution.py:27
  92.3 1.4 fusion.16
  93.7 16.0 %psum.22 = f32[32,32]{0,1:T(8,128)S(1)} all-reduce(f32[32,32]{0,1:T(8,128)S(1)} %fusion.16), channel_id=1, replica_groups=mesh['replica'=8,'shard'=4] {'shard'}, use_global_device_ids=true, to_apply=%region_1.2 | all-reduce | flops 1024 | bytes 8192 | tf_op jit(solution)/shard_map/psum | solution.py:29
  109.9 2.9 cholesky.16
  112.8 0.6 compare_reduce_fusion
  113.4 4.1 %collective-permute-done.4 = bf16[2048,64]{0,1:T(8,128)(2,1)} collective-permute-done((bf16[2048,64]{0,1:T(8,128)(2,1)S(1)}, bf16[2048,64]{0,1:T(8,128)(2,1)}, u32[]{:S(2)}, u32[]{:S(2)}) %collective-permute-start.4) | collective-permute-done | bytes 262176 | tf_op jit(solution)/shard_map/ppermute | solution.py:17
  117.5 0.7 fusion.21
  118.2 2.4 custom-call.7
  120.6 1.4 fusion.14
  122.0 3.4 %collective-permute-done.5 = bf16[2048,64]{0,1:T(8,128)(2,1)} collective-permute-done((bf16[2048,64]{0,1:T(8,128)(2,1)}, bf16[2048,64]{0,1:T(8,128)(2,1)}, u32[]{:S(2)}, u32[]{:S(2)}) %collective-permute-start.5) | collective-permute-done | bytes 262176 | tf_op jit(solution)/shard_map/ppermute | solution.py:17
  125.4 6.4 %fusion.8 = f32[512,32]{1,0:T(8,128)} fusion(f32[32,2048]{1,0:T(8,128)S(1)} %fusion.14, bf16[2048,512]{0,1:T(8,128)(2,1)} %copy.10, bf16[1,2048,512]{1,2,0:T(8,128)(2,1)} %copy.12, bf16[1,2048,512]{1,2,0:T(8,128)(2,1)} %copy.11), kind=kOutput, calls=%fused_computation.10 | convolution fusion | flops 407896064 | bytes 6619136 | tf_op jit(solution)/shard_map/dot_general | solution.py:32
  131.9 0.2 reduce-scatter.2.cloned.1.call-start
  132.1 1.3 collective-permute-done.6
  133.4 1.7 constant_dynamic-update-slice_fusion.15
  135.0 1.7 constant_dynamic-update-slice_fusion.14
  136.7 1.7 constant_dynamic-update-slice_fusion.13
  138.4 1.7 constant_dynamic-update-slice_fusion.12
  140.0 0.7 constant_dynamic-update-slice_fusion.11
  140.7 0.7 constant_dynamic-update-slice_fusion.10
  141.5 0.7 constant_dynamic-update-slice_fusion.9
  142.2 0.7 constant_dynamic-update-slice_fusion.8
  142.9 1.7 constant_dynamic-update-slice_fusion.7
  144.6 1.7 constant_dynamic-update-slice_fusion.6
  146.2 1.7 constant_dynamic-update-slice_fusion.5
  147.9 0.7 constant_dynamic-update-slice_fusion.4
  148.6 0.7 constant_dynamic-update-slice_fusion.3
  149.4 0.7 constant_dynamic-update-slice_fusion.2
  150.1 0.7 constant_dynamic-update-slice_fusion.1
  150.8 0.7 constant_dynamic-update-slice_fusion
  151.5 106.4 %all-reduce.5.cloned.1.call-done = f32[512,32]{1,0:T(8,128)} async-done(((f32[512,32]{1,0:T(8,128)}), f32[512,32]{1,0:T(8,128)}) %all-reduce.5.cloned.1.call-update) | async-done | bytes 65552 | tf_op jit(solution)/shard_map/psum | solution.py:33
  257.9 6.3 %multiply_add_fusion = (bf16[2048,512]{0,1:T(8,128)(2,1)}, f32[2048,512]{0,1:T(8,128)S(1)}) fusion(bf16[2048,1024]{0,1:T(8,128)(2,1)} %constant_dynamic-update-slice_fusion, s32[]{:T(128)S(6)} %select_n.21, f32[32,2048]{1,0:T(8,128)S(1)} %fusion.14, f32[512,32]{1,0:T(8,128)} %all-reduce.5.cloned.1.call-done), kind=kOutput, calls=%fused_computation.5 | convolution fusion | flops 406863872 | bytes 8716292 | tf_op jit(solution)/shard_map/dot_general | solution.py:34
  264.2 4.7 %fusion.2 = (bf16[1,2048,512]{1,2,0:T(8,128)(2,1)}, bf16[2048,512]{0,1:T(8,128)(2,1)S(1)}) fusion(f32[2048,512]{0,1:T(8,128)S(1)} %get-tuple-element.11, bf16[1,2048,512]{1,2,0:T(8,128)(2,1)S(1)} %copy-done.3, bf16[1,2048,512]{1,2,0:T(8,128)(2,1)S(1)} %copy-done.1, bf16[2048,512]{0,1:T(8,128)(2,1)S(1)} %copy-done.2, ...), kind=kLoop, calls=%fused_computation.6 | loop fusion | flops 15728640 | bytes 16777220 | tf_op jit(solution)/shard_map/broadcast_in_dim | solution.py:35
  268.9 1.3 copy-done.4
  270.3 2.2 fusion.5
  272.5 3.9 %copy.15 = bf16[2048,512]{1,0:T(8,128)(2,1)} copy(bf16[2048,512]{0,1:T(8,128)(2,1)} %copy-done.4) | data formatting | bytes 4194304
  276.5 3.9 %copy.16 = bf16[1,2048,512]{2,1,0:T(8,128)(2,1)} copy(bf16[1,2048,512]{1,2,0:T(8,128)(2,1)} %get-tuple-element.8) | data formatting | bytes 4194304
  280.4 1.7 dynamic-slice_convert_fusion
  282.1 17.6 %reduce-scatter.2.cloned.1.call-done = f32[128,512]{0,1:T(8,128)} async-done(((f32[512,512]{0,1:T(8,128)}), f32[128,512]{0,1:T(8,128)}) %reduce-scatter.2.cloned.1.call-update) | async-done | bytes 262160 | tf_op jit(solution)/shard_map/reduce_scatter | solution.py:45
  299.7 1.0 convert_bitcast_fusion
  300.6 0.8 copy.17
  (32 shorter events, 0.4 us)
Async XLA Ops:
  7.2 263.1 %copy-start = (bf16[1,512,2048]{2,1,0:T(8,128)(2,1)S(1)}, bf16[1,512,2048]{2,1,0:T(8,128)(2,1)}, u32[]{:S(2)}) copy-start(bf16[1,512,2048]{2,1,0:T(8,128)(2,1)} %param.11) | copy-start | bytes 6291460
  7.2 85.2 %all-reduce.3.cloned.1.call-start = ((), (), s32[]{:S(2)}) async-start(), calls=%async_computation.1 | async-start | bytes 524288 | tf_op jit(solution)/shard_map/psum | solution.py:27
  7.2 8.8 %collective-permute-start = (bf16[2048,64]{0,1:T(8,128)(2,1)}, bf16[2048,64]{0,1:T(8,128)(2,1)S(1)}, u32[]{:S(2)}, u32[]{:S(2)}) collective-permute-start(bf16[2048,64]{0,1:T(8,128)(2,1)} %param.8), channel_id=1, source_target_pairs={{0,4},{4,8},{8,12},{12,16},{16,20},{20,24},{24,28},{28,0},{1,5},{5... | collective-permute-start | bytes 786440 | tf_op jit(solution)/shard_map/ppermute | solution.py:17
  16.1 11.8 %collective-permute-start.1 = (bf16[2048,64]{0,1:T(8,128)(2,1)S(1)}, bf16[2048,64]{0,1:T(8,128)(2,1)S(1)}, u32[]{:S(2)}, u32[]{:S(2)}) collective-permute-start(bf16[2048,64]{0,1:T(8,128)(2,1)S(1)} %collective-permute-done), channel_id=1, source_target_pairs={{0,4},{4,8},{8,12},{12,16},{16,20},{20,24},{24,28},{28,0},{1,5},{5... | collective-permute-start | bytes 786440 | tf_op jit(solution)/shard_map/ppermute | solution.py:17
  20.0 8.2 %copy-start.8 = (f32[512,32]{0,1:T(8,128)S(1)}, f32[512,32]{0,1:T(8,128)}, u32[]{:S(2)}) copy-start(f32[512,32]{0,1:T(8,128)} %param.10) | copy-start | bytes 196612
  27.9 7.6 %collective-permute-start.2 = (bf16[2048,64]{0,1:T(8,128)(2,1)S(1)}, bf16[2048,64]{0,1:T(8,128)(2,1)S(1)}, u32[]{:S(2)}, u32[]{:S(2)}) collective-permute-start(bf16[2048,64]{0,1:T(8,128)(2,1)S(1)} %collective-permute-done.1), channel_id=1, source_target_pairs={{0,4},{4,8},{8,12},{12,16},{16,20},{20,24},{24,28},{28,0},{1,5},{5... | collective-permute-start | bytes 786440 | tf_op jit(solution)/shard_map/ppermute | solution.py:17
  35.1 222.9 %all-reduce.5.cloned.1.call-start = ((), (), s32[]{:S(2)}) async-start(), calls=%async_computation.2 | async-start | bytes 524288 | tf_op jit(solution)/shard_map/psum | solution.py:33
  35.5 74.3 %collective-permute-start.3 = (bf16[2048,64]{0,1:T(8,128)(2,1)S(1)}, bf16[2048,64]{0,1:T(8,128)(2,1)S(1)}, u32[]{:S(2)}, u32[]{:S(2)}) collective-permute-start(bf16[2048,64]{0,1:T(8,128)(2,1)S(1)} %collective-permute-done.2), channel_id=1, source_target_pairs={{0,4},{4,8},{8,12},{12,16},{16,20},{20,24},{24,28},{28,0},{1,5},{5... | collective-permute-start | bytes 786440 | tf_op jit(solution)/shard_map/ppermute | solution.py:17
  109.8 8.4 %copy-start.6 = (bf16[2048,64]{0,1:T(8,128)(2,1)}, bf16[2048,64]{0,1:T(8,128)(2,1)S(1)}, u32[]{:S(2)}) copy-start(bf16[2048,64]{0,1:T(8,128)(2,1)S(1)} %collective-permute-done.3) | copy-start | bytes 786436
  109.8 7.7 %collective-permute-start.4 = (bf16[2048,64]{0,1:T(8,128)(2,1)S(1)}, bf16[2048,64]{0,1:T(8,128)(2,1)}, u32[]{:S(2)}, u32[]{:S(2)}) collective-permute-start(bf16[2048,64]{0,1:T(8,128)(2,1)S(1)} %collective-permute-done.3), channel_id=1, source_target_pairs={{0,4},{4,8},{8,12},{12,16},{16,20},{20,24},{24,28},{28,0},{1,5},{5... | collective-permute-start | bytes 786440 | tf_op jit(solution)/shard_map/ppermute | solution.py:17
  117.5 7.9 %collective-permute-start.5 = (bf16[2048,64]{0,1:T(8,128)(2,1)}, bf16[2048,64]{0,1:T(8,128)(2,1)}, u32[]{:S(2)}, u32[]{:S(2)}) collective-permute-start(bf16[2048,64]{0,1:T(8,128)(2,1)} %collective-permute-done.4), channel_id=1, source_target_pairs={{0,4},{4,8},{8,12},{12,16},{16,20},{20,24},{24,28},{28,0},{1,5},{5... | collective-permute-start | bytes 786440 | tf_op jit(solution)/shard_map/ppermute | solution.py:17
  122.0 20.1 %copy-start.5 = (bf16[2048,64]{0,1:T(8,128)(2,1)S(1)}, bf16[2048,64]{0,1:T(8,128)(2,1)}, u32[]{:S(2)}) copy-start(bf16[2048,64]{0,1:T(8,128)(2,1)} %param.8) | copy-start | bytes 786436
  125.4 7.9 %collective-permute-start.6 = (bf16[2048,64]{0,1:T(8,128)(2,1)}, bf16[2048,64]{0,1:T(8,128)(2,1)}, u32[]{:S(2)}, u32[]{:S(2)}) collective-permute-start(bf16[2048,64]{0,1:T(8,128)(2,1)} %collective-permute-done.5), channel_id=1, source_target_pairs={{0,4},{4,8},{8,12},{12,16},{16,20},{20,24},{24,28},{28,0},{1,5},{5... | collective-permute-start | bytes 786440 | tf_op jit(solution)/shard_map/ppermute | solution.py:17
  131.9 167.8 %reduce-scatter.2.cloned.1.call-start = ((), (), s32[]{:S(2)}) async-start(), calls=%async_computation.3 | async-start | bytes 1310720 | tf_op jit(solution)/shard_map/reduce_scatter | solution.py:45
  132.1 15.8 %copy-start.7 = (bf16[2048,64]{0,1:T(8,128)(2,1)S(1)}, bf16[2048,64]{0,1:T(8,128)(2,1)}, u32[]{:S(2)}) copy-start(bf16[2048,64]{0,1:T(8,128)(2,1)} %copy-done.6) | copy-start | bytes 786436
  257.9 6.3 %copy-start.1 = (bf16[1,2048,512]{1,2,0:T(8,128)(2,1)S(1)}, bf16[1,2048,512]{1,2,0:T(8,128)(2,1)}, u32[]{:S(2)}) copy-start(bf16[1,2048,512]{1,2,0:T(8,128)(2,1)} %copy.11) | copy-start | bytes 6291460
  257.9 6.3 %copy-start.2 = (bf16[2048,512]{0,1:T(8,128)(2,1)S(1)}, bf16[2048,512]{0,1:T(8,128)(2,1)}, u32[]{:S(2)}) copy-start(bf16[2048,512]{0,1:T(8,128)(2,1)} %copy.10) | copy-start | bytes 6291460
  257.9 6.3 %copy-start.3 = (bf16[1,2048,512]{1,2,0:T(8,128)(2,1)S(1)}, bf16[1,2048,512]{1,2,0:T(8,128)(2,1)}, u32[]{:S(2)}) copy-start(bf16[1,2048,512]{1,2,0:T(8,128)(2,1)} %copy.12) | copy-start | bytes 6291460
  268.9 1.3 copy-start.4
Sparse Core Ops, SparseCore 0:
  35.2 57.1 all-reduce.2
  132.0 125.9 all-reduce.4
  272.7 26.9 reduce-scatter.1
